TPU v7x, 512 devices: a whole 4x8x8 slice. The times are simulated.
512 devices in a mesh: cluster: 64 (over y, z), copy: 8 (over x, core).
Axes of the slice: x: 4, y: 8, z: 8, core: 2. Of those that a mesh axis runs over, the one named last changes fastest.
Arguments:
- points: bfloat16 [8192, 128, 512], P(('cluster', 'copy')), may hold values from -18 to 18
- block_ids: int32 [8192], P(('cluster', 'copy')), may hold values from 0 to 63, as said below
- block_counts: int32 [512], P(('cluster', 'copy')), may hold values from 11 to 16, as said below
- centroids: bfloat16 [131072, 512], P('cluster'), may hold values from -6 to 6
Outputs:
- new_centroids: bfloat16 [131072, 512], P(('cluster', 'copy'))
Inputs may be any that keep to these rules, and one draw needn't show every extreme that they name: `block_ids`: the 16 blocks of one device name 16 different coarse clusters. For every index along copy, one coarse cluster is named by the first block of every device with that copy index. Only the first block_counts[d] block slots of device d are valid. Some device has all 16 valid.
All inputs are finite; a program needn't handle non-finite values.
Results may differ from a plain program's by a relative error of at most 0.0021.
Values may be sent and summed in bfloat16 or wider, within the bound.
A program may use at most 64 MiB of HBM per device.

v0:
```python
import math

import jax
import jax.numpy as jnp
from jax import lax
from jax.sharding import PartitionSpec as P

turn_blocks = 4


def owner_sums(received, arrived, centroids):
    slot_total = received.shape[0]
    block_rows = received.shape[1]
    feature = received.shape[2]
    present = arrived > 0.5
    how_many = jnp.sum(present.astype(jnp.int32))
    ranking = jnp.cumsum(present.astype(jnp.int32)) - 1
    listing = jnp.zeros((slot_total + turn_blocks,), jnp.int32)
    listing = listing.at[jnp.where(present, ranking, slot_total + turn_blocks)].set(
        jnp.arange(slot_total, dtype=jnp.int32), mode="drop"
    )
    scale_factor = 3.0 / math.sqrt(feature)

    def visit(step_index, running):
        start_at = step_index * turn_blocks
        chosen = lax.dynamic_slice_in_dim(listing, start_at, turn_blocks)
        usable = start_at + jnp.arange(turn_blocks, dtype=jnp.int32) < how_many
        gathered = received[chosen].reshape(turn_blocks * block_rows, feature)
        logits = (
            jnp.einsum("rd,kd->rk", gathered, centroids, preferred_element_type=jnp.float32)
            * scale_factor
        )
        row_mask = jnp.repeat(usable, block_rows).astype(jnp.float32)[:, None]
        weights = (jax.nn.softmax(logits, axis=-1) * row_mask).astype(jnp.bfloat16)
        return running + jnp.einsum(
            "rk,rd->kd", weights, gathered, preferred_element_type=jnp.float32
        )

    initial = jnp.zeros((centroids.shape[0], feature), jnp.float32)
    return lax.fori_loop(0, (how_many + turn_blocks - 1) // turn_blocks, visit, initial)


def local(points, block_ids, block_counts, centroids):
    held = points.shape[0]
    owners = lax.axis_size("cluster")
    in_range = jnp.arange(held, dtype=jnp.int32) < block_counts[0]
    routing = jnp.where(in_range, block_ids, -1).astype(jnp.bfloat16)
    targets = routing.astype(jnp.int32)
    slot_index = jnp.arange(held, dtype=jnp.int32)
    matches = targets[None, :] == jnp.arange(owners, dtype=jnp.int32)[:, None]
    present = jnp.any(matches, axis=1)
    position = jnp.sum(jnp.where(matches, slot_index[None, :], 0), axis=1)
    outgoing = jnp.where(present[:, None, None], points[position], jnp.zeros((), jnp.bfloat16))
    received, arrived = (
        lax.all_to_all(outgoing, "cluster", split_axis=0, concat_axis=0, tiled=True),
        lax.all_to_all(
            present.astype(jnp.bfloat16), "cluster", split_axis=0, concat_axis=0, tiled=True
        ),
    )
    partial_sums = owner_sums(received, arrived, centroids)
    share = lax.psum_scatter(partial_sums, "copy", scatter_dimension=0, tiled=True)
    share_rows = share.shape[0]
    previous = lax.dynamic_slice_in_dim(
        centroids, lax.axis_index("copy") * share_rows, share_rows, 0
    ).astype(jnp.float32)
    combined = share + previous
    scaled = combined * lax.rsqrt(jnp.mean(combined * combined, axis=-1, keepdims=True) + 1e-06)
    return scaled.astype(jnp.bfloat16)


def solution(mesh):
    return jax.shard_map(
        local,
        mesh=mesh,
        in_specs=(
            P(("cluster", "copy"), None, None),
            P(("cluster", "copy")),
            P(("cluster", "copy")),
            P("cluster", None),
        ),
        out_specs=P(("cluster", "copy"), None),
        check_vma=False,
    )
```

profile of v0, /device:TPU:1, one launch (start us, length us, event | category | flops | bytes accessed | tf_op | source)
XLA Modules:
  0.0 598.5 jit_solution(12431081177450282385)
XLA Ops:
  8.8 17.1 %all-to-all-start = ((bf16[64,1,1]{2,1,0:T(2,128)(2,1)}), bf16[64,1,1]{2,1,0:T(2,128)(2,1)S(1)}, u32[]{:S(2)}, u32[]{:S(2)}) async-start(bf16[64,1,1]{2,1,0:T(2,128)(2,1)} %copy.27), calls=%async_computation | async-start | bytes 65536 | tf_op jit(solution)/shard_map/all_to_all | solution.py:56
  26.3 5.3 gather_fusion.1
  31.6 7.2 %broadcast_select_fusion = bf16[64,128,512]{2,1,0:T(8,128)(2,1)} fusion(bf16[64,128,512]{2,1,0:T(8,128)(2,1)} %gather_fusion.1, pred[64]{0:T(512)(128)(4,1)S(1)} %fusion.8), kind=kLoop, calls=%fused_computation.16 | loop fusion | flops 4194304 | bytes 16777280 | tf_op jit(solution)/shard_map/jit(_where)/select_n | solution.py:53
  38.9 12.4 %all-to-all-start.1 = ((bf16[64,128,512]{2,1,0:T(8,128)(2,1)}), bf16[64,128,512]{2,1,0:T(8,128)(2,1)}, u32[]{:S(2)}, u32[]{:S(2)}) async-start(bf16[64,128,512]{2,1,0:T(8,128)(2,1)} %broadcast_select_fusion), calls=%async_computation.1 | async-start | bytes 16777216 | tf_op jit(solution)/shard_map/all_to_all | solution.py:55
  55.1 245.9 %all-to-all-done.1 = bf16[64,128,512]{2,1,0:T(8,128)(2,1)} async-done(((bf16[64,128,512]{2,1,0:T(8,128)(2,1)}), bf16[64,128,512]{2,1,0:T(8,128)(2,1)}, u32[]{:S(2)}, u32[]{:S(2)}) %all-to-all-start.1) | async-done | bytes 8388640 | tf_op jit(solution)/shard_map/all_to_all | solution.py:55
  303.5 86.6 %while.10 = (s32[]{:T(128)}, f32[2048,512]{1,0:T(8,128)}, s32[]{:T(128)}, s32[68]{0:T(128)S(1)}, bf16[64,128,512]{2,1,0:T(8,128)(2,1)}, /*index=5*/bf16[2048,512...) while((s32[]{:T(128)}, f32[2048,512]{1,0:T(8,128)}, s32[]{:T(128)}, ...), condition=%wide.region_8.9_spmd, body=%wide.region_5.8_spmd.sunk | while | flops 2159017984 | bytes 25184520 | solution.py:40
  303.6 4.0 gather_fusion
  307.6 3.0 multiply_reduce_fusion.3
  312.0 5.9 convolution_add_fusion.2
  318.0 4.0 gather_fusion
  322.0 3.0 multiply_reduce_fusion.3
  326.4 5.9 convolution_add_fusion.2
  332.5 4.0 gather_fusion
  336.4 3.0 multiply_reduce_fusion.3
  340.9 5.9 convolution_add_fusion.2
  346.9 4.0 gather_fusion
  350.9 3.0 multiply_reduce_fusion.3
  355.3 5.9 convolution_add_fusion.2
  361.3 4.0 gather_fusion
  365.3 3.0 multiply_reduce_fusion.3
  369.7 5.9 convolution_add_fusion.2
  375.8 4.0 gather_fusion
  384.2 5.9 convolution_add_fusion.2
  390.2 198.4 %reduce-scatter.2.cloned.1.call-done = f32[256,512]{1,0:T(8,128)} async-done(((f32[2048,512]{1,0:T(8,128)}), f32[256,512]{1,0:T(8,128)}) %reduce-scatter.2.cloned.1.call-update) | async-done | bytes 524304 | tf_op jit(solution)/shard_map/reduce_scatter | solution.py:61
  (57 shorter events, 22.9 us)
Async XLA Ops:
  6.5 19.8 %copy-start = (bf16[16,128,512]{2,1,0:T(8,128)(2,1)S(1)}, bf16[16,128,512]{2,1,0:T(8,128)(2,1)}, u32[]{:S(2)}) copy-start(bf16[16,128,512]{2,1,0:T(8,128)(2,1)} %param.6) | copy-start | bytes 6291460
  8.8 30.0 %all-to-all-start = ((bf16[64,1,1]{2,1,0:T(2,128)(2,1)}), bf16[64,1,1]{2,1,0:T(2,128)(2,1)S(1)}, u32[]{:S(2)}, u32[]{:S(2)}) async-start(bf16[64,1,1]{2,1,0:T(2,128)(2,1)} %copy.27), calls=%async_computation | async-start | bytes 65536 | tf_op jit(solution)/shard_map/all_to_all | solution.py:56
  38.9 262.2 %all-to-all-start.1 = ((bf16[64,128,512]{2,1,0:T(8,128)(2,1)}), bf16[64,128,512]{2,1,0:T(8,128)(2,1)}, u32[]{:S(2)}, u32[]{:S(2)}) async-start(bf16[64,128,512]{2,1,0:T(8,128)(2,1)} %broadcast_select_fusion), calls=%async_computation.1 | async-start | bytes 16777216 | tf_op jit(solution)/shard_map/all_to_all | solution.py:55
  51.3 537.2 %reduce-scatter.2.cloned.1.call-start = ((), (), s32[]{:S(2)}) async-start(), calls=%async_computation.3 | async-start | bytes 4718592 | tf_op jit(solution)/shard_map/reduce_scatter | solution.py:61
Sparse Core Ops, SparseCore 0:
  390.3 198.2 reduce-scatter.1
where the time goes:
time: 602 us; the launch traced here: 599 us
  waiting for transfers between devices  444 us (74%)
  matrix products  53.5 us (9%)
  local copies, waits for them, and re-layouts  33.9 us (6%)
  starting transfers between devices  29.6 us (5%)
  other arithmetic  22.4 us (4%)
  between operations  14.9 us (2%)
    all_to_all x1, waiting for transfers between devices, local(): lax.all_to_all(outgoing, 'cluster', split_axis=0, concat_axis=0, tiled=True)  246 us
    reduce_scatter x1, waiting for transfers between devices, local(): lax.psum_scatter(partial_sums, 'copy', scatter_dimension=0, tiled=True)  198 us
    dot_general x6, matrix products, visit(): jnp.einsum('rk,rd->kd', weights, gathered, preferred_element_type=jnp.flo...  35.7 us
    gather x6, local copies, waits for them, and re-layouts, visit(): gathered = received[chosen].reshape(turn_blocks * block_rows, feature)  23.8 us
    dot_general x6, matrix products, visit(): jnp.einsum('rd,kd->rk', gathered, centroids, preferred_element_type=jnp.f...  17.8 us
    all_to_all x1, starting transfers between devices, local(): lax.all_to_all(present.astype(jnp.bfloat16), 'cluster', split_axis=0, con...  17.1 us
    all_to_all x1, starting transfers between devices, local(): lax.all_to_all(outgoing, 'cluster', split_axis=0, concat_axis=0, tiled=True)  12.4 us
  transfers between devices with their start and end apart: 3, of which 2 were waited for; matrix products, arithmetic and copies ran while one was open for 3% of the time, Pallas kernels for 0%

commit v1 on v0

v1 whole, which is shorter than its diff:
```python
import functools
import math

import jax
import jax.numpy as jnp
from jax import lax
from jax.experimental import pallas as pl
from jax.experimental.pallas import tpu as pltpu
from jax.sharding import PartitionSpec as P

MESH = pl.DeviceIdType.MESH
GROUP = 4
STRIDE = 27
TILE = 256


def kernel(
    shape, pos_ref, flag_ref, pts_ref, cent_ref, out_ref,
    stage, recv, logit, acc, pair, sbuf, rbuf,
    send_sem, recv_sem, pair_send, pair_recv, ring_send, ring_recv,
):
    slots, side, copies = shape
    rows, feature = cent_ref.shape
    share = rows // copies
    chips = copies // 2
    me = lax.axis_index("cluster")
    lane = lax.axis_index("copy")
    row, col = me // side, me % side
    chip, core = lane // 2, lane % 2
    partner = chip * 2 + (1 - core)

    def target(q):
        offset = (q * STRIDE) % slots
        return ((row + offset // side) % side) * side + (col + offset % side) % side

    barrier = pltpu.get_barrier_semaphore()

    def greet(q, carry):
        pl.semaphore_signal(barrier, inc=1, device_id=(target(q), lane), device_id_type=MESH)
        return carry

    lax.fori_loop(1, slots, greet, 0)
    pl.semaphore_signal(barrier, inc=1, device_id=(me, partner), device_id_type=MESH)
    for d in range(1, chips):
        other = ((chip + d) % chips) * 2 + core
        pl.semaphore_signal(barrier, inc=1, device_id=(me, other), device_id_type=MESH)

    recv[0] = pts_ref[pos_ref[me]] * flag_ref[me].astype(jnp.bfloat16)

    def fill(q, carry):
        k = target(q)
        stage[q] = pts_ref[pos_ref[k]] * flag_ref[k].astype(jnp.bfloat16)
        return carry

    lax.fori_loop(1, slots, fill, 0)
    acc[...] = jnp.zeros_like(acc)
    pl.semaphore_wait(barrier, slots - 1 + chips)

    def exchange(q):
        return pltpu.make_async_remote_copy(
            src_ref=stage.at[q],
            dst_ref=recv.at[q],
            send_sem=send_sem.at[q],
            recv_sem=recv_sem.at[q],
            device_id=(target(q), lane),
            device_id_type=MESH,
        )

    def begin(q, carry):
        exchange(q).start()
        return carry

    lax.fori_loop(1, slots, begin, 0)

    alpha = 3.0 / math.sqrt(feature) * math.log2(math.e)
    points = GROUP * pts_ref.shape[1]

    def step(j, carry):
        def arrive(b, carry):
            exchange(j * GROUP + b).wait_recv()
            return carry

        lax.fori_loop(jnp.where(j == 0, 1, 0), GROUP, arrive, 0)

        def block():
            return recv[pl.ds(j * GROUP, GROUP)].reshape(points, feature)

        def scores(r, top):
            at = pl.ds(pl.multiple_of(r * TILE, TILE), TILE)
            part = lax.dot_general(
                cent_ref[at, :], block(), (((1,), (1,)), ((), ())),
                preferred_element_type=jnp.float32,
            )
            logit[at, :] = part
            return jnp.maximum(top, jnp.max(part, axis=0, keepdims=True))

        top = lax.fori_loop(
            0, rows // TILE, scores, jnp.full((1, points), -jnp.inf, jnp.float32)
        ) * alpha

        def powers(r, total):
            at = pl.ds(pl.multiple_of(r * TILE, TILE), TILE)
            value = jnp.exp2(logit[at, :] * alpha - top)
            logit[at, :] = value
            return total + jnp.sum(value, axis=0, keepdims=True)

        total = lax.fori_loop(0, rows // TILE, powers, jnp.zeros((1, points), jnp.float32))
        inverse = 1.0 / total

        def add(r, carry):
            at = pl.ds(pl.multiple_of(r * TILE, TILE), TILE)
            weights = (logit[at, :] * inverse).astype(jnp.bfloat16)
            acc[at, :] += jnp.dot(weights, block(), preferred_element_type=jnp.float32)
            return carry

        lax.fori_loop(0, rows // TILE, add, 0)
        return carry

    lax.fori_loop(0, slots // GROUP, step, 0)

    def across(t, other_core):
        at = pl.ds(pl.multiple_of((2 * t + other_core) * share, share), share)
        return pltpu.make_async_remote_copy(
            src_ref=acc.at[at, :],
            dst_ref=pair.at[t],
            send_sem=pair_send.at[t],
            recv_sem=pair_recv.at[t],
            device_id=(me, partner),
            device_id_type=MESH,
        )

    def ring(d):
        return pltpu.make_async_remote_copy(
            src_ref=sbuf.at[d - 1],
            dst_ref=rbuf.at[d - 1],
            send_sem=ring_send.at[d - 1],
            recv_sem=ring_recv.at[d - 1],
            device_id=(me, ((chip + d) % chips) * 2 + core),
            device_id_type=MESH,
        )

    order = [2, 1, 3, 0][:chips]
    for d in order:
        across((chip + d) % chips, 1 - core).start()
    for d in order:
        t = (chip + d) % chips
        across(t, 1 - core).wait_recv()
        if d:
            at = pl.ds(pl.multiple_of((2 * t + core) * share, share), share)
            sbuf[d - 1] = (acc[at, :] + pair[t]).astype(jnp.bfloat16)
            ring(d).start()
    mine = pl.ds(pl.multiple_of(lane * share, share), share)
    value = acc[mine, :] + pair[chip] + cent_ref[mine, :].astype(jnp.float32)
    for d in order:
        if d:
            ring(d).wait_recv()
            value = value + rbuf[d - 1].astype(jnp.float32)
    scale = lax.rsqrt(jnp.mean(value * value, axis=-1, keepdims=True) + 1e-06)
    out_ref[...] = (value * scale).astype(jnp.bfloat16)

    def finish(q, carry):
        exchange(q).wait_send()
        return carry

    lax.fori_loop(1, slots, finish, 0)
    for d in order:
        across((chip + d) % chips, 1 - core).wait_send()
        if d:
            ring(d).wait_send()


def local(points, block_ids, block_counts, centroids):
    held, block_rows, feature = points.shape
    slots = lax.axis_size("cluster")
    copies = lax.axis_size("copy")
    rows = centroids.shape[0]
    share = rows // copies
    chips = copies // 2
    slot_index = jnp.arange(held, dtype=jnp.int32)
    matches = (block_ids[None, :] == jnp.arange(slots, dtype=jnp.int32)[:, None]) & (
        slot_index < block_counts[0]
    )[None, :]
    flag = jnp.any(matches, axis=1).astype(jnp.float32)
    position = jnp.sum(jnp.where(matches, slot_index[None, :], 0), axis=1).astype(jnp.int32)
    smem = pl.BlockSpec(memory_space=pltpu.SMEM)
    vmem = pl.BlockSpec(memory_space=pltpu.VMEM)
    blocks = (slots, block_rows, feature)
    dma = pltpu.SemaphoreType.DMA
    return pl.pallas_call(
        functools.partial(kernel, (slots, int(math.sqrt(slots)), copies)),
        out_shape=jax.ShapeDtypeStruct((share, feature), jnp.bfloat16),
        in_specs=[smem, smem, vmem, vmem],
        out_specs=vmem,
        scratch_shapes=[
            pltpu.VMEM(blocks, jnp.bfloat16),
            pltpu.VMEM(blocks, jnp.bfloat16),
            pltpu.VMEM((rows, GROUP * block_rows), jnp.float32),
            pltpu.VMEM((rows, feature), jnp.float32),
            pltpu.VMEM((chips, share, feature), jnp.float32),
            pltpu.VMEM((chips - 1, share, feature), jnp.bfloat16),
            pltpu.VMEM((chips - 1, share, feature), jnp.bfloat16),
            dma((slots,)),
            dma((slots,)),
            dma((chips,)),
            dma((chips,)),
            dma((chips - 1,)),
            dma((chips - 1,)),
        ],
        compiler_params=pltpu.CompilerParams(
            collective_id=0, has_side_effects=True, vmem_limit_bytes=56 << 20
        ),
    )(position, flag, points, centroids)


def solution(mesh):
    return jax.shard_map(
        local,
        mesh=mesh,
        in_specs=(
            P(("cluster", "copy"), None, None),
            P(("cluster", "copy")),
            P(("cluster", "copy")),
            P("cluster", None),
        ),
        out_specs=P(("cluster", "copy"), None),
        check_vma=False,
    )
```

time: 602 us -> 324 us (0.54)
  the two profiles are of different devices: /device:TPU:1 before, /device:TPU:43 now
where the time goes in v1:
time: 324 us
  Pallas kernels  319 us (98%)
    pallas_call x1, Pallas kernels, local(): pl.pallas_call(functools.partial(kernel, (slots, int(math.sqrt(slots)), c...  319 us

profile of v1, /device:TPU:43, one launch (start us, length us, event | category | flops | bytes accessed | tf_op | source)
XLA Modules:
  0.0 323.5 jit_solution(11303708779595879509)
XLA Ops:
  0.7 0.7 fusion.1
  1.4 1.3 select_reduce_fusion.pos_ref
  2.7 0.6 convert_element_type.3.flag_ref
  3.2 318.6 %shard_map.46 = bf16[256,512]{1,0:T(8,128)(2,1)} custom-call(s32[64]{0:T(128)} %select_reduce_fusion.pos_ref, f32[64]{0:T(128)} %convert_element_type.3.flag_ref, bf16[16,128,512]{2,1,0:T(8,128)(2,1)} %pts_ref.1, bf16[2048,512]{1,0:T(8,128)(2,1)} %cent_ref.1), custom_call_target="tpu_custom_call" | custom-call | tf_op jit(solution)/shard_map/pallas_call | solution.py:189
  321.8 1.7 copy.7
  (1 shorter events, 0.0 us)

commit v2 on v1

--- a/solution.py
+++ b/solution.py
@@ -10,14 +10,15 @@
 
 MESH = pl.DeviceIdType.MESH
 GROUP = 4
-STRIDE = 27
+LEAD = 2
+BATCH = 8
 TILE = 256
 
 
 def kernel(
     shape, pos_ref, flag_ref, pts_ref, cent_ref, out_ref,
-    stage, recv, logit, acc, pair, sbuf, rbuf,
-    send_sem, recv_sem, pair_send, pair_recv, ring_send, ring_recv,
+    stage, mid, recv, logit, acc, pair, sbuf, rbuf,
+    send_sem, mid_sem, relay_sem, recv_sem, pair_send, pair_recv, ring_send, ring_recv,
 ):
     slots, side, copies = shape
     rows, feature = cent_ref.shape
@@ -29,17 +30,33 @@
     chip, core = lane // 2, lane % 2
     partner = chip * 2 + (1 - core)
 
-    def target(q):
-        offset = (q * STRIDE) % slots
-        return ((row + offset // side) % side) * side + (col + offset % side) % side
+    def ranked(a):
+        return jnp.where(a % 2 == 0, 1 + a // 2, side - 1 - a // 2)
+
+    def at_offset(dy, dz):
+        return ((row + dy) % side) * side + (col + dz) % side
+
+    def direct(q):
+        d = ranked(q // 2)
+        return jnp.where(q % 2 == 0, d, 0), jnp.where(q % 2 == 0, 0, d)
+
+    def turning(r):
+        dy = ranked(r % (side - 1))
+        dz = ranked((r // (side - 1) + r) % (side - 1))
+        return dy, dz, (dy + dz) % 2 == 0
+
+    straight = 2 * (side - 1)
+    relays = (side - 1) * (side - 1)
 
     barrier = pltpu.get_barrier_semaphore()
 
     def greet(q, carry):
-        pl.semaphore_signal(barrier, inc=1, device_id=(target(q), lane), device_id_type=MESH)
-        return carry
-
-    lax.fori_loop(1, slots, greet, 0)
+        pl.semaphore_signal(
+            barrier, inc=1, device_id=(at_offset(*direct(q)), lane), device_id_type=MESH
+        )
+        return carry
+
+    lax.fori_loop(0, straight, greet, 0)
     pl.semaphore_signal(barrier, inc=1, device_id=(me, partner), device_id_type=MESH)
     for d in range(1, chips):
         other = ((chip + d) % chips) * 2 + core
@@ -47,37 +64,87 @@
 
     recv[0] = pts_ref[pos_ref[me]] * flag_ref[me].astype(jnp.bfloat16)
 
-    def fill(q, carry):
-        k = target(q)
-        stage[q] = pts_ref[pos_ref[k]] * flag_ref[k].astype(jnp.bfloat16)
-        return carry
-
-    lax.fori_loop(1, slots, fill, 0)
+    def fill(slot, k):
+        stage[slot] = pts_ref[pos_ref[k]] * flag_ref[k].astype(jnp.bfloat16)
+
+    def fill_straight(q, carry):
+        fill(q, at_offset(*direct(q)))
+        return carry
+
+    def fill_turning(r, carry):
+        dy, dz, _ = turning(r)
+        fill(straight + r, at_offset(dy, dz))
+        return carry
+
+    lax.fori_loop(0, straight, fill_straight, 0)
+    lax.fori_loop(0, relays, fill_turning, 0)
     acc[...] = jnp.zeros_like(acc)
-    pl.semaphore_wait(barrier, slots - 1 + chips)
-
-    def exchange(q):
+    pl.semaphore_wait(barrier, straight + chips)
+
+    def go(q):
         return pltpu.make_async_remote_copy(
             src_ref=stage.at[q],
-            dst_ref=recv.at[q],
+            dst_ref=recv.at[1 + q],
             send_sem=send_sem.at[q],
-            recv_sem=recv_sem.at[q],
-            device_id=(target(q), lane),
-            device_id_type=MESH,
-        )
-
-    def begin(q, carry):
-        exchange(q).start()
-        return carry
-
-    lax.fori_loop(1, slots, begin, 0)
+            recv_sem=recv_sem.at[1 + q],
+            device_id=(at_offset(*direct(q)), lane),
+            device_id_type=MESH,
+        )
+
+    def first(r):
+        dy, dz, along_y = turning(r)
+        return pltpu.make_async_remote_copy(
+            src_ref=stage.at[straight + r],
+            dst_ref=mid.at[r],
+            send_sem=send_sem.at[straight + r],
+            recv_sem=mid_sem.at[r],
+            device_id=(
+                at_offset(jnp.where(along_y, dy, 0), jnp.where(along_y, 0, dz)), lane
+            ),
+            device_id_type=MESH,
+        )
+
+    def second(r):
+        dy, dz, along_y = turning(r)
+        return pltpu.make_async_remote_copy(
+            src_ref=mid.at[r],
+            dst_ref=recv.at[1 + straight + r],
+            send_sem=relay_sem.at[r],
+            recv_sem=recv_sem.at[1 + straight + r],
+            device_id=(
+                at_offset(jnp.where(along_y, 0, dy), jnp.where(along_y, dz, 0)), lane
+            ),
+            device_id_type=MESH,
+        )
+
+    def begin_straight(q, carry):
+        go(q).start()
+        return carry
+
+    def begin_turning(r, carry):
+        first(r).start()
+        return carry
+
+    def relay(r, carry):
+        first(r).wait_recv()
+        second(r).start()
+        return carry
+
+    lax.fori_loop(0, straight, begin_straight, 0)
+    lax.fori_loop(0, relays, begin_turning, 0)
 
     alpha = 3.0 / math.sqrt(feature) * math.log2(math.e)
     points = GROUP * pts_ref.shape[1]
 
+    def relayed(j):
+        return jnp.clip((j - LEAD) * BATCH, 0, relays)
+
     def step(j, carry):
+        lax.fori_loop(relayed(j), relayed(j + 1), relay, 0)
+
         def arrive(b, carry):
-            exchange(j * GROUP + b).wait_recv()
+            slot = j * GROUP + b
+            pltpu.make_async_copy(recv.at[slot], recv.at[slot], recv_sem.at[slot]).wait()
             return carry
 
         lax.fori_loop(jnp.where(j == 0, 1, 0), GROUP, arrive, 0)
@@ -158,11 +225,17 @@
     scale = lax.rsqrt(jnp.mean(value * value, axis=-1, keepdims=True) + 1e-06)
     out_ref[...] = (value * scale).astype(jnp.bfloat16)
 
-    def finish(q, carry):
-        exchange(q).wait_send()
-        return carry
-
-    lax.fori_loop(1, slots, finish, 0)
+    def finish_straight(q, carry):
+        go(q).wait_send()
+        return carry
+
+    def finish_turning(r, carry):
+        first(r).wait_send()
+        second(r).wait_send()
+        return carry
+
+    lax.fori_loop(0, straight, finish_straight, 0)
+    lax.fori_loop(0, relays, finish_turning, 0)
     for d in order:
         across((chip + d) % chips, 1 - core).wait_send()
         if d:
@@ -184,22 +257,27 @@
     position = jnp.sum(jnp.where(matches, slot_index[None, :], 0), axis=1).astype(jnp.int32)
     smem = pl.BlockSpec(memory_space=pltpu.SMEM)
     vmem = pl.BlockSpec(memory_space=pltpu.VMEM)
+    side = int(math.sqrt(slots))
+    relays = (side - 1) * (side - 1)
     blocks = (slots, block_rows, feature)
     dma = pltpu.SemaphoreType.DMA
     return pl.pallas_call(
-        functools.partial(kernel, (slots, int(math.sqrt(slots)), copies)),
+        functools.partial(kernel, (slots, side, copies)),
         out_shape=jax.ShapeDtypeStruct((share, feature), jnp.bfloat16),
         in_specs=[smem, smem, vmem, vmem],
         out_specs=vmem,
         scratch_shapes=[
-            pltpu.VMEM(blocks, jnp.bfloat16),
+            pltpu.VMEM((slots - 1, block_rows, feature), jnp.bfloat16),
+            pltpu.VMEM((relays, block_rows, feature), jnp.bfloat16),
             pltpu.VMEM(blocks, jnp.bfloat16),
             pltpu.VMEM((rows, GROUP * block_rows), jnp.float32),
             pltpu.VMEM((rows, feature), jnp.float32),
             pltpu.VMEM((chips, share, feature), jnp.float32),
             pltpu.VMEM((chips - 1, share, feature), jnp.bfloat16),
             pltpu.VMEM((chips - 1, share, feature), jnp.bfloat16),
-            dma((slots,)),
+            dma((slots - 1,)),
+            dma((relays,)),
+            dma((relays,)),
             dma((slots,)),
             dma((chips,)),
             dma((chips,)),

time: 324 us -> 247 us (0.76)
  the two profiles are of different devices: /device:TPU:43 before, /device:TPU:1 now
where the time goes in v2:
time: 247 us; the launch traced here: 243 us
  Pallas kernels  238 us (96%)
  other arithmetic  2.58 us (1%)
    pallas_call x1, Pallas kernels, local(): pl.pallas_call(functools.partial(kernel, (slots, side, copies)), out_shap...  238 us

profile of v2, /device:TPU:1, one launch (start us, length us, event | category | flops | bytes accessed | tf_op | source)
XLA Modules:
  0.0 242.9 jit_solution(4593660443926399641)
XLA Ops:
  0.7 0.7 fusion.1
  1.4 1.3 select_reduce_fusion.pos_ref
  2.7 0.6 convert_element_type.3.flag_ref
  3.2 238.0 %shard_map.46 = bf16[256,512]{1,0:T(8,128)(2,1)} custom-call(s32[64]{0:T(128)} %select_reduce_fusion.pos_ref, f32[64]{0:T(128)} %convert_element_type.3.flag_ref, bf16[16,128,512]{2,1,0:T(8,128)(2,1)} %pts_ref.1, bf16[2048,512]{1,0:T(8,128)(2,1)} %cent_ref.1), custom_call_target="tpu_custom_call" | custom-call | tf_op jit(solution)/shard_map/pallas_call | solution.py:264
  241.2 1.7 copy.7
  (1 shorter events, 0.0 us)

commit v3 on v2

--- a/solution.py
+++ b/solution.py
@@ -10,15 +10,15 @@
 
 MESH = pl.DeviceIdType.MESH
 GROUP = 4
-LEAD = 2
-BATCH = 8
-TILE = 256
+LEAD = 1
+BATCH = 17
+TILE = 512
 
 
 def kernel(
-    shape, pos_ref, flag_ref, pts_ref, cent_ref, out_ref,
-    stage, mid, recv, logit, acc, pair, sbuf, rbuf,
-    send_sem, mid_sem, relay_sem, recv_sem, pair_send, pair_recv, ring_send, ring_recv,
+    shape, ids_ref, count_ref, points_ref, centroids_ref, out_ref,
+    pts_ref, cent_ref, stage, mid, recv, logit, acc, pair, sbuf, rbuf,
+    send_sem, mid_sem, relay_sem, recv_sem, pair_send, pair_recv, ring_send, ring_recv, load_sem,
 ):
     slots, side, copies = shape
     rows, feature = cent_ref.shape
@@ -48,6 +48,11 @@
     straight = 2 * (side - 1)
     relays = (side - 1) * (side - 1)
 
+    load_points = pltpu.make_async_copy(points_ref, pts_ref, load_sem.at[0])
+    load_centroids = pltpu.make_async_copy(centroids_ref, cent_ref, load_sem.at[1])
+    load_points.start()
+    load_centroids.start()
+
     barrier = pltpu.get_barrier_semaphore()
 
     def greet(q, carry):
@@ -62,23 +67,25 @@
         other = ((chip + d) % chips) * 2 + core
         pl.semaphore_signal(barrier, inc=1, device_id=(me, other), device_id_type=MESH)
 
-    recv[0] = pts_ref[pos_ref[me]] * flag_ref[me].astype(jnp.bfloat16)
-
-    def fill(slot, k):
-        stage[slot] = pts_ref[pos_ref[k]] * flag_ref[k].astype(jnp.bfloat16)
+    count = count_ref[0]
+    held = pts_ref.shape[0]
+
+    def routed(k):
+        found = jnp.int32(0)
+        where = jnp.int32(0)
+        for n in range(held):
+            hit = jnp.where(ids_ref[n] == k, 1, 0) * jnp.where(count > n, 1, 0)
+            found = found + hit
+            where = where + n * hit
+        return pts_ref[where] * found.astype(jnp.float32).astype(jnp.bfloat16)
+
+    load_points.wait()
 
     def fill_straight(q, carry):
-        fill(q, at_offset(*direct(q)))
-        return carry
-
-    def fill_turning(r, carry):
-        dy, dz, _ = turning(r)
-        fill(straight + r, at_offset(dy, dz))
+        stage[q] = routed(at_offset(*direct(q)))
         return carry
 
     lax.fori_loop(0, straight, fill_straight, 0)
-    lax.fori_loop(0, relays, fill_turning, 0)
-    acc[...] = jnp.zeros_like(acc)
     pl.semaphore_wait(barrier, straight + chips)
 
     def go(q):
@@ -122,6 +129,8 @@
         return carry
 
     def begin_turning(r, carry):
+        dy, dz, _ = turning(r)
+        stage[straight + r] = routed(at_offset(dy, dz))
         first(r).start()
         return carry
 
@@ -132,6 +141,9 @@
 
     lax.fori_loop(0, straight, begin_straight, 0)
     lax.fori_loop(0, relays, begin_turning, 0)
+    recv[0] = routed(me)
+    acc[...] = jnp.zeros_like(acc)
+    load_centroids.wait()
 
     alpha = 3.0 / math.sqrt(feature) * math.log2(math.e)
     points = GROUP * pts_ref.shape[1]
@@ -139,7 +151,7 @@
     def relayed(j):
         return jnp.clip((j - LEAD) * BATCH, 0, relays)
 
-    def step(j, carry):
+    def ready(j):
         lax.fori_loop(relayed(j), relayed(j + 1), relay, 0)
 
         def arrive(b, carry):
@@ -149,21 +161,23 @@
 
         lax.fori_loop(jnp.where(j == 0, 1, 0), GROUP, arrive, 0)
 
-        def block():
-            return recv[pl.ds(j * GROUP, GROUP)].reshape(points, feature)
-
+    def block(j):
+        return recv[pl.ds(j * GROUP, GROUP)].reshape(points, feature)
+
+    def tiles(function, initial):
+        return lax.fori_loop(0, rows // TILE, function, initial, unroll=True)
+
+    def exponentials(j):
         def scores(r, top):
             at = pl.ds(pl.multiple_of(r * TILE, TILE), TILE)
             part = lax.dot_general(
-                cent_ref[at, :], block(), (((1,), (1,)), ((), ())),
+                cent_ref[at, :], block(j), (((1,), (1,)), ((), ())),
                 preferred_element_type=jnp.float32,
             )
             logit[at, :] = part
             return jnp.maximum(top, jnp.max(part, axis=0, keepdims=True))
 
-        top = lax.fori_loop(
-            0, rows // TILE, scores, jnp.full((1, points), -jnp.inf, jnp.float32)
-        ) * alpha
+        top = tiles(scores, jnp.full((1, points), -jnp.inf, jnp.float32)) * alpha
 
         def powers(r, total):
             at = pl.ds(pl.multiple_of(r * TILE, TILE), TILE)
@@ -171,19 +185,27 @@
             logit[at, :] = value
             return total + jnp.sum(value, axis=0, keepdims=True)
 
-        total = lax.fori_loop(0, rows // TILE, powers, jnp.zeros((1, points), jnp.float32))
-        inverse = 1.0 / total
-
-        def add(r, carry):
-            at = pl.ds(pl.multiple_of(r * TILE, TILE), TILE)
-            weights = (logit[at, :] * inverse).astype(jnp.bfloat16)
-            acc[at, :] += jnp.dot(weights, block(), preferred_element_type=jnp.float32)
+        return 1.0 / tiles(powers, jnp.zeros((1, points), jnp.float32))
+
+    def add(j, at, inverse):
+        weights = (logit[at, :] * inverse).astype(jnp.bfloat16)
+        acc[at, :] += jnp.dot(weights, block(j), preferred_element_type=jnp.float32)
+
+    def step(j, carry):
+        ready(j)
+        inverse = exponentials(j)
+
+        def sums(r, carry):
+            add(j, pl.ds(pl.multiple_of(r * TILE, TILE), TILE), inverse)
             return carry
 
-        lax.fori_loop(0, rows // TILE, add, 0)
-        return carry
-
-    lax.fori_loop(0, slots // GROUP, step, 0)
+        tiles(sums, 0)
+        return carry
+
+    last = slots // GROUP - 1
+    lax.fori_loop(0, last, step, 0)
+    ready(last)
+    inverse = exponentials(last)
 
     def across(t, other_core):
         at = pl.ds(pl.multiple_of((2 * t + other_core) * share, share), share)
@@ -206,15 +228,20 @@
             device_id_type=MESH,
         )
 
+    def chunk(t, of_core):
+        return pl.ds(pl.multiple_of((2 * t + of_core) * share, share), share)
+
     order = [2, 1, 3, 0][:chips]
     for d in order:
-        across((chip + d) % chips, 1 - core).start()
+        t = (chip + d) % chips
+        add(last, chunk(t, 1 - core), inverse)
+        across(t, 1 - core).start()
     for d in order:
         t = (chip + d) % chips
+        add(last, chunk(t, core), inverse)
         across(t, 1 - core).wait_recv()
         if d:
-            at = pl.ds(pl.multiple_of((2 * t + core) * share, share), share)
-            sbuf[d - 1] = (acc[at, :] + pair[t]).astype(jnp.bfloat16)
+            sbuf[d - 1] = (acc[chunk(t, core), :] + pair[t]).astype(jnp.bfloat16)
             ring(d).start()
     mine = pl.ds(pl.multiple_of(lane * share, share), share)
     value = acc[mine, :] + pair[chip] + cent_ref[mine, :].astype(jnp.float32)
@@ -249,13 +276,8 @@
     rows = centroids.shape[0]
     share = rows // copies
     chips = copies // 2
-    slot_index = jnp.arange(held, dtype=jnp.int32)
-    matches = (block_ids[None, :] == jnp.arange(slots, dtype=jnp.int32)[:, None]) & (
-        slot_index < block_counts[0]
-    )[None, :]
-    flag = jnp.any(matches, axis=1).astype(jnp.float32)
-    position = jnp.sum(jnp.where(matches, slot_index[None, :], 0), axis=1).astype(jnp.int32)
     smem = pl.BlockSpec(memory_space=pltpu.SMEM)
+    anywhere = pl.BlockSpec(memory_space=pl.ANY)
     vmem = pl.BlockSpec(memory_space=pltpu.VMEM)
     side = int(math.sqrt(slots))
     relays = (side - 1) * (side - 1)
@@ -264,9 +286,11 @@
     return pl.pallas_call(
         functools.partial(kernel, (slots, side, copies)),
         out_shape=jax.ShapeDtypeStruct((share, feature), jnp.bfloat16),
-        in_specs=[smem, smem, vmem, vmem],
+        in_specs=[smem, smem, anywhere, anywhere],
         out_specs=vmem,
         scratch_shapes=[
+            pltpu.VMEM(points.shape, jnp.bfloat16),
+            pltpu.VMEM(centroids.shape, jnp.bfloat16),
             pltpu.VMEM((slots - 1, block_rows, feature), jnp.bfloat16),
             pltpu.VMEM((relays, block_rows, feature), jnp.bfloat16),
             pltpu.VMEM(blocks, jnp.bfloat16),
@@ -283,11 +307,12 @@
             dma((chips,)),
             dma((chips - 1,)),
             dma((chips - 1,)),
+            dma((2,)),
         ],
         compiler_params=pltpu.CompilerParams(
             collective_id=0, has_side_effects=True, vmem_limit_bytes=56 << 20
         ),
-    )(position, flag, points, centroids)
+    )(block_ids, block_counts, points, centroids)
 
 
 def solution(mesh):

time: 247 us -> 230 us (0.931)
  Pallas kernels: 238 us -> 223 us
  other arithmetic: 2.58 us -> 0 us
    pallas_call x1, Pallas kernels: 238 us -> 223 us  [local(): pl.pallas_call(functools.partial(kernel, (slots, side, copies)), out_shap...]
where the time goes in v3:
time: 230 us; the launch traced here: 226 us
  Pallas kernels  223 us (97%)
    pallas_call x1, Pallas kernels, local(): pl.pallas_call(functools.partial(kernel, (slots, side, copies)), out_shap...  223 us

profile of v3, /device:TPU:1, one launch (start us, length us, event | category | flops | bytes accessed | tf_op | source)
XLA Modules:
  0.0 225.8 jit_solution(9533989070893049053)
XLA Ops:
  0.7 223.4 %shard_map.46 = bf16[256,512]{1,0:T(8,128)(2,1)} custom-call(s32[16]{0:T(128)} %ids_ref.1, s32[1]{0:T(128)S(6)} %copy.6.count_ref, bf16[16,128,512]{2,1,0:T(8,128)(2,1)} %points_ref.1, bf16[2048,512]{1,0:T(8,128)(2,1)} %centroids_ref.1), custom_call_target="tpu_custom_call" | custom-call | tf_op jit(solution)/shard_map/pallas_call | solution.py:286
  224.1 1.7 copy.7

commit v4 on v3

v4 whole, which is shorter than its diff:
```python
import functools
import math

import jax
import jax.numpy as jnp
from jax import lax
from jax.experimental import pallas as pl
from jax.experimental.pallas import tpu as pltpu
from jax.sharding import PartitionSpec as P

MESH = pl.DeviceIdType.MESH
GROUP = 4
TILE = 512


def kernel(
    shape, ids_ref, count_ref, points_ref, centroids_ref, out_ref,
    pts_ref, cent_ref, raw1_up, raw1_down, raw2_up, raw2_down, picked, land3, land4,
    stage, recv, names, logit, acc, pair, sbuf, rbuf,
    near_send, near_recv, name_send, name_recv, far_send, far_recv,
    pair_send, pair_recv, ring_send, ring_recv, load_sem,
):
    slots, side, copies = shape
    rows, feature = cent_ref.shape
    held = pts_ref.shape[0]
    half = held // 2
    share = rows // copies
    chips = copies // 2
    me = lax.axis_index("cluster")
    lane = lax.axis_index("copy")
    chip, core = lane // 2, lane % 2
    partner = chip * 2 + (1 - core)
    u = (1 - core) * (me // side) + core * (me % side)
    v = (1 - core) * (me % side) + core * (me // side)

    def at_offset(du, dv):
        a, b = (u + du + side) % side, (v + dv + side) % side
        return (1 - core) * (a * side + b) + core * (b * side + a)

    def ranked(i):
        return jnp.where(i % 2 == 1, (i + 1) // 2, (side - i // 2) % side)

    load_points = pltpu.make_async_copy(points_ref, pts_ref, load_sem.at[0])
    load_centroids = pltpu.make_async_copy(centroids_ref, cent_ref, load_sem.at[1])
    load_points.start()
    load_centroids.start()

    barrier = pltpu.get_barrier_semaphore()

    def signal(cluster, copy):
        pl.semaphore_signal(barrier, inc=1, device_id=(cluster, copy), device_id_type=MESH)

    for d in (1, -1, 2, -2):
        signal(at_offset(d, 0), lane)

    def greet(d, carry):
        signal(at_offset(0, d), lane)
        return carry

    lax.fori_loop(1, side, greet, 0)
    signal(me, partner)
    for d in range(1, chips):
        signal(me, ((chip + d) % chips) * 2 + core)

    count = count_ref[0]
    column = lax.broadcasted_iota(jnp.int32, names.shape[1:], 1)
    listed = jnp.full(names.shape[1:], -1, jnp.int32)
    for n in range(held):
        listed = jnp.where(column == n, jnp.where(count > n, ids_ref[n], -1), listed)
    names[0] = listed

    def pick(source, entry, k):
        code = jnp.max(jnp.where(names[entry] == k, column + 1, 0))
        found = jnp.minimum(code, 1).astype(jnp.float32).astype(jnp.bfloat16)
        return source[jnp.maximum(code - 1, 0)] * found

    def send(src, dst, send_sem, recv_sem, cluster):
        return pltpu.make_async_remote_copy(
            src_ref=src,
            dst_ref=dst,
            send_sem=send_sem,
            recv_sem=recv_sem,
            device_id=(cluster, lane),
            device_id_type=MESH,
        )

    raw1, raw2 = (raw1_up, raw1_down), (raw2_up, raw2_down)
    sign = (1, -1)
    part = [pl.ds(0, half), pl.ds(half, half)]

    def tell(p, d):
        at = 2 * (d - 1) + p
        return send(
            names.at[0], names.at[1 + at], name_send.at[at], name_recv.at[at],
            at_offset(sign[p] * d, 0),
        )

    def hop1(p, h):
        return send(
            pts_ref.at[part[h]], raw1[p].at[part[h]],
            near_send.at[7 * p + h], near_recv.at[7 * p + h], at_offset(sign[p], 0),
        )

    def hop2(p, h):
        return send(
            raw1[p].at[part[h]], raw2[p].at[part[h]],
            near_send.at[7 * p + 2 + h], near_recv.at[7 * p + 2 + h], at_offset(sign[p], 0),
        )

    hop3_parts = [pl.ds(0, side // 2), pl.ds(side // 2, side)]

    def hop3(p, h):
        return send(
            picked.at[p, hop3_parts[h]], land3.at[p, hop3_parts[h]],
            near_send.at[7 * p + 4 + h], near_recv.at[7 * p + 4 + h], at_offset(sign[p], 0),
        )

    def hop4(p):
        return send(
            land3.at[p, hop3_parts[0]], land4.at[p],
            near_send.at[7 * p + 6], near_recv.at[7 * p + 6], at_offset(sign[p], 0),
        )

    sources = [pts_ref, raw1_up, raw1_down, raw2_up, raw2_down]

    def held_at(o, i):
        if o < 5:
            return stage.at[o, i]
        if o < 7:
            return land3.at[o - 5, side // 2 + i]
        return land4.at[i // (side // 2), i % (side // 2)]

    def across_v(o, i):
        return send(
            held_at(o, i), recv.at[o * side + i],
            far_send.at[o * side + i], far_recv.at[o * side + i], at_offset(0, ranked(i)),
        )

    def spread(o):
        def one(i, carry):
            if o < 5:
                stage[o, i] = pick(sources[o], o, at_offset(0, ranked(i)))
            across_v(o, i).start()
            return carry

        lax.fori_loop(1, side, one, 0)
        if o < 5:
            recv[o * side] = pick(sources[o], o, me)
        elif o < 7:
            recv[o * side] = land3[o - 5, side // 2]
        else:
            recv[o * side] = land4[0, 0]

    load_points.wait()
    pl.semaphore_wait(barrier, 4 + side - 1 + chips)
    both = (0, 1)
    for p in both:
        for d in (1, 2):
            tell(p, d).start()
    for h in both:
        for p in both:
            hop1(p, h).start()
    spread(0)
    acc[...] = jnp.zeros_like(acc)
    load_centroids.wait()

    def events(j):
        @pl.when(j == 0)
        def _():
            for p in both:
                hop1(p, 0).wait_recv()
                hop2(p, 0).start()

        @pl.when(j == 1)
        def _():
            for p in both:
                hop1(p, 1).wait_recv()
                hop2(p, 1).start()
            for p in both:
                tell(p, 1).wait_recv()
                spread(1 + p)

        @pl.when(j == 3)
        def _():
            for p in both:
                tell(p, 2).wait_recv()
                hop2(p, 0).wait_recv()
                hop2(p, 1).wait_recv()

                def beyond(i, carry):
                    k = at_offset(2 * sign[p], ranked(p * (side // 2) + i))
                    picked[p, i] = pick(raw2[p], 3 + p, k)
                    return carry

                def following(i, carry):
                    k = at_offset(sign[p], ranked(i))
                    picked[p, side // 2 + i] = pick(raw2[p], 3 + p, k)
                    return carry

                lax.fori_loop(0, side // 2, beyond, 0)
                hop3(p, 0).start()
                lax.fori_loop(0, side, following, 0)
                hop3(p, 1).start()
            for p in both:
                spread(3 + p)

        @pl.when(j == 6)
        def _():
            for p in both:
                hop3(p, 0).wait_recv()
                hop4(p).start()
            for p in both:
                hop3(p, 1).wait_recv()
                spread(5 + p)

        @pl.when(j == 8)
        def _():
            for p in both:
                hop4(p).wait_recv()
            spread(7)

    alpha = 3.0 / math.sqrt(feature) * math.log2(math.e)
    points = GROUP * pts_ref.shape[1]

    def ready(j):
        events(j)

        def arrive(b, carry):
            slot = j * GROUP + b
            pltpu.make_async_copy(recv.at[slot], recv.at[slot], far_recv.at[slot]).wait()
            return carry

        lax.fori_loop(jnp.where((j * GROUP) % side == 0, 1, 0), GROUP, arrive, 0)

    def block(j):
        return recv[pl.ds(j * GROUP, GROUP)].reshape(points, feature)

    def tiles(function, initial):
        return lax.fori_loop(0, rows // TILE, function, initial, unroll=True)

    def exponentials(j):
        def scores(r, top):
            at = pl.ds(pl.multiple_of(r * TILE, TILE), TILE)
            part = lax.dot_general(
                cent_ref[at, :], block(j), (((1,), (1,)), ((), ())),
                preferred_element_type=jnp.float32,
            )
            logit[at, :] = part
            return jnp.maximum(top, jnp.max(part, axis=0, keepdims=True))

        top = tiles(scores, jnp.full((1, points), -jnp.inf, jnp.float32)) * alpha

        def powers(r, total):
            at = pl.ds(pl.multiple_of(r * TILE, TILE), TILE)
            value = jnp.exp2(logit[at, :] * alpha - top)
            logit[at, :] = value
            return total + jnp.sum(value, axis=0, keepdims=True)

        return 1.0 / tiles(powers, jnp.zeros((1, points), jnp.float32))

    def add(j, at, inverse):
        weights = (logit[at, :] * inverse).astype(jnp.bfloat16)
        acc[at, :] += jnp.dot(weights, block(j), preferred_element_type=jnp.float32)

    def step(j, carry):
        ready(j)
        inverse = exponentials(j)

        def sums(r, carry):
            add(j, pl.ds(pl.multiple_of(r * TILE, TILE), TILE), inverse)
            return carry

        tiles(sums, 0)
        return carry

    last = slots // GROUP - 1
    lax.fori_loop(0, last, step, 0)
    ready(last)
    inverse = exponentials(last)

    def across(t, other_core):
        at = pl.ds(pl.multiple_of((2 * t + other_core) * share, share), share)
        return pltpu.make_async_remote_copy(
            src_ref=acc.at[at, :],
            dst_ref=pair.at[t],
            send_sem=pair_send.at[t],
            recv_sem=pair_recv.at[t],
            device_id=(me, partner),
            device_id_type=MESH,
        )

    def ring(d):
        return pltpu.make_async_remote_copy(
            src_ref=sbuf.at[d - 1],
            dst_ref=rbuf.at[d - 1],
            send_sem=ring_send.at[d - 1],
            recv_sem=ring_recv.at[d - 1],
            device_id=(me, ((chip + d) % chips) * 2 + core),
            device_id_type=MESH,
        )

    def chunk(t, of_core):
        return pl.ds(pl.multiple_of((2 * t + of_core) * share, share), share)

    order = [2, 1, 3, 0][:chips]
    for d in order:
        t = (chip + d) % chips
        add(last, chunk(t, 1 - core), inverse)
        across(t, 1 - core).start()
    for d in order:
        t = (chip + d) % chips
        add(last, chunk(t, core), inverse)
        across(t, 1 - core).wait_recv()
        if d:
            sbuf[d - 1] = (acc[chunk(t, core), :] + pair[t]).astype(jnp.bfloat16)
            ring(d).start()
    mine = pl.ds(pl.multiple_of(lane * share, share), share)
    value = acc[mine, :] + pair[chip] + cent_ref[mine, :].astype(jnp.float32)
    for d in order:
        if d:
            ring(d).wait_recv()
            value = value + rbuf[d - 1].astype(jnp.float32)
    scale = lax.rsqrt(jnp.mean(value * value, axis=-1, keepdims=True) + 1e-06)
    out_ref[...] = (value * scale).astype(jnp.bfloat16)

    for p in both:
        for h in both:
            tell(p, 1 + h).wait_send()
            hop1(p, h).wait_send()
            hop2(p, h).wait_send()
            hop3(p, h).wait_send()
        hop4(p).wait_send()
    for o in range(side):

        def sent(i, carry):
            across_v(o, i).wait_send()
            return carry

        lax.fori_loop(1, side, sent, 0)
    for d in order:
        across((chip + d) % chips, 1 - core).wait_send()
        if d:
            ring(d).wait_send()


def local(points, block_ids, block_counts, centroids):
    held, block_rows, feature = points.shape
    slots = lax.axis_size("cluster")
    copies = lax.axis_size("copy")
    rows = centroids.shape[0]
    share = rows // copies
    chips = copies // 2
    smem = pl.BlockSpec(memory_space=pltpu.SMEM)
    anywhere = pl.BlockSpec(memory_space=pl.ANY)
    vmem = pl.BlockSpec(memory_space=pltpu.VMEM)
    side = int(math.sqrt(slots))
    def blocks(*lead):
        return pltpu.VMEM((*lead, block_rows, feature), jnp.bfloat16)

    dma = pltpu.SemaphoreType.DMA
    return pl.pallas_call(
        functools.partial(kernel, (slots, side, copies)),
        out_shape=jax.ShapeDtypeStruct((share, feature), jnp.bfloat16),
        in_specs=[smem, smem, anywhere, anywhere],
        out_specs=vmem,
        scratch_shapes=[
            pltpu.VMEM(points.shape, jnp.bfloat16),
            pltpu.VMEM(centroids.shape, jnp.bfloat16),
            blocks(held),
            blocks(held),
            blocks(held),
            blocks(held),
            blocks(2, side + side // 2),
            blocks(2, side + side // 2),
            blocks(2, side // 2),
            blocks(5, side),
            blocks(slots),
            pltpu.VMEM((5, 8, 128), jnp.int32),
            pltpu.VMEM((rows, GROUP * block_rows), jnp.float32),
            pltpu.VMEM((rows, feature), jnp.float32),
            pltpu.VMEM((chips, share, feature), jnp.float32),
            pltpu.VMEM((chips - 1, share, feature), jnp.bfloat16),
            pltpu.VMEM((chips - 1, share, feature), jnp.bfloat16),
            dma((14,)),
            dma((14,)),
            dma((4,)),
            dma((4,)),
            dma((slots,)),
            dma((slots,)),
            dma((chips,)),
            dma((chips,)),
            dma((chips - 1,)),
            dma((chips - 1,)),
            dma((2,)),
        ],
        compiler_params=pltpu.CompilerParams(
            collective_id=0, has_side_effects=True, vmem_limit_bytes=56 << 20
        ),
    )(block_ids, block_counts, points, centroids)


def solution(mesh):
    return jax.shard_map(
        local,
        mesh=mesh,
        in_specs=(
            P(("cluster", "copy"), None, None),
            P(("cluster", "copy")),
            P(("cluster", "copy")),
            P("cluster", None),
        ),
        out_specs=P(("cluster", "copy"), None),
        check_vma=False,
    )
```

time: 230 us -> 216 us (0.939)
  the two profiles are of different devices: /device:TPU:1 before, /device:TPU:465 now
where the time goes in v4:
time: 216 us
  Pallas kernels  213 us (99%)
    pallas_call x1, Pallas kernels, local(): pl.pallas_call(functools.partial(kernel, (slots, side, copies)), out_shap...  213 us

profile of v4, /device:TPU:465, one launch (start us, length us, event | category | flops | bytes accessed | tf_op | source)
XLA Modules:
  0.0 215.8 jit_solution(15775750774878600425)
XLA Ops:
  0.7 213.5 %shard_map.46 = bf16[256,512]{1,0:T(8,128)(2,1)} custom-call(s32[16]{0:T(128)} %ids_ref.1, s32[1]{0:T(128)S(6)} %copy.6.count_ref, bf16[16,128,512]{2,1,0:T(8,128)(2,1)} %points_ref.1, bf16[2048,512]{1,0:T(8,128)(2,1)} %centroids_ref.1), custom_call_target="tpu_custom_call" | custom-call | tf_op jit(solution)/shard_map/pallas_call | solution.py:361
  214.1 1.7 copy.7

commit v5 on v4

--- a/solution.py
+++ b/solution.py
@@ -160,71 +160,48 @@
     for h in both:
         for p in both:
             hop1(p, h).start()
-    spread(0)
     acc[...] = jnp.zeros_like(acc)
     load_centroids.wait()
-
-    def events(j):
-        @pl.when(j == 0)
-        def _():
-            for p in both:
-                hop1(p, 0).wait_recv()
-                hop2(p, 0).start()
-
-        @pl.when(j == 1)
-        def _():
-            for p in both:
-                hop1(p, 1).wait_recv()
-                hop2(p, 1).start()
-            for p in both:
-                tell(p, 1).wait_recv()
-                spread(1 + p)
-
-        @pl.when(j == 3)
-        def _():
-            for p in both:
-                tell(p, 2).wait_recv()
-                hop2(p, 0).wait_recv()
-                hop2(p, 1).wait_recv()
-
-                def beyond(i, carry):
-                    k = at_offset(2 * sign[p], ranked(p * (side // 2) + i))
-                    picked[p, i] = pick(raw2[p], 3 + p, k)
-                    return carry
-
-                def following(i, carry):
-                    k = at_offset(sign[p], ranked(i))
-                    picked[p, side // 2 + i] = pick(raw2[p], 3 + p, k)
-                    return carry
-
-                lax.fori_loop(0, side // 2, beyond, 0)
-                hop3(p, 0).start()
-                lax.fori_loop(0, side, following, 0)
-                hop3(p, 1).start()
-            for p in both:
-                spread(3 + p)
-
-        @pl.when(j == 6)
-        def _():
-            for p in both:
-                hop3(p, 0).wait_recv()
-                hop4(p).start()
-            for p in both:
-                hop3(p, 1).wait_recv()
-                spread(5 + p)
-
-        @pl.when(j == 8)
-        def _():
-            for p in both:
-                hop4(p).wait_recv()
-            spread(7)
+    for h in both:
+        for p in both:
+            hop1(p, h).wait_recv()
+            hop2(p, h).start()
+    for p in both:
+        tell(p, 2).wait_recv()
+        hop2(p, 0).wait_recv()
+        hop2(p, 1).wait_recv()
+
+        def beyond(i, carry):
+            k = at_offset(2 * sign[p], ranked(p * (side // 2) + i))
+            picked[p, i] = pick(raw2[p], 3 + p, k)
+            return carry
+
+        def following(i, carry):
+            k = at_offset(sign[p], ranked(i))
+            picked[p, side // 2 + i] = pick(raw2[p], 3 + p, k)
+            return carry
+
+        lax.fori_loop(0, side // 2, beyond, 0)
+        hop3(p, 0).start()
+        lax.fori_loop(0, side, following, 0)
+        hop3(p, 1).start()
+    for p in both:
+        hop3(p, 0).wait_recv()
+        hop4(p).start()
+    for p in both:
+        tell(p, 1).wait_recv()
+        hop3(p, 1).wait_recv()
+    spread(0)
+    spread(1)
+    for p in both:
+        hop4(p).wait_recv()
+    for o in range(2, side):
+        spread(o)
 
     alpha = 3.0 / math.sqrt(feature) * math.log2(math.e)
     points = GROUP * pts_ref.shape[1]
 
     def ready(j):
-        events(j)
-
         def arrive(b, carry):
             slot = j * GROUP + b
             pltpu.make_async_copy(recv.at[slot], recv.at[slot], far_recv.at[slot]).wait()
@@ -314,15 +291,6 @@
         if d:
             sbuf[d - 1] = (acc[chunk(t, core), :] + pair[t]).astype(jnp.bfloat16)
             ring(d).start()
-    mine = pl.ds(pl.multiple_of(lane * share, share), share)
-    value = acc[mine, :] + pair[chip] + cent_ref[mine, :].astype(jnp.float32)
-    for d in order:
-        if d:
-            ring(d).wait_recv()
-            value = value + rbuf[d - 1].astype(jnp.float32)
-    scale = lax.rsqrt(jnp.mean(value * value, axis=-1, keepdims=True) + 1e-06)
-    out_ref[...] = (value * scale).astype(jnp.bfloat16)
-
     for p in both:
         for h in both:
             tell(p, 1 + h).wait_send()
@@ -339,6 +307,16 @@
         lax.fori_loop(1, side, sent, 0)
     for d in order:
         across((chip + d) % chips, 1 - core).wait_send()
+    mine = pl.ds(pl.multiple_of(lane * share, share), share)
+    value = acc[mine, :] + pair[chip] + cent_ref[mine, :].astype(jnp.float32)
+    for d in order:
+        if d:
+            ring(d).wait_recv()
+            value = value + rbuf[d - 1].astype(jnp.float32)
+    scale = lax.rsqrt(jnp.mean(value * value, axis=-1, keepdims=True) + 1e-06)
+    out_ref[...] = (value * scale).astype(jnp.bfloat16)
+
+    for d in order:
         if d:
             ring(d).wait_send()
 

time: 216 us -> 205 us (0.949)
  the two profiles are of different devices: /device:TPU:465 before, /device:TPU:1 now
where the time goes in v5:
time: 205 us; the launch traced here: 203 us
  Pallas kernels  201 us (98%)
    pallas_call x1, Pallas kernels, local(): pl.pallas_call(functools.partial(kernel, (slots, side, copies)), out_shap...  201 us

profile of v5, /device:TPU:1, one launch (start us, length us, event | category | flops | bytes accessed | tf_op | source)
XLA Modules:
  0.0 203.3 jit_solution(17228112942708186938)
XLA Ops:
  0.7 201.0 %shard_map.46 = bf16[256,512]{1,0:T(8,128)(2,1)} custom-call(s32[16]{0:T(128)} %ids_ref.1, s32[1]{0:T(128)S(6)} %copy.6.count_ref, bf16[16,128,512]{2,1,0:T(8,128)(2,1)} %points_ref.1, bf16[2048,512]{1,0:T(8,128)(2,1)} %centroids_ref.1), custom_call_target="tpu_custom_call" | custom-call | tf_op jit(solution)/shard_map/pallas_call | solution.py:339
  201.6 1.7 copy.7

commit v6 on v5

--- a/solution.py
+++ b/solution.py
@@ -97,7 +97,7 @@
 
     def hop1(p, h):
         return send(
-            pts_ref.at[part[h]], raw1[p].at[part[h]],
+            points_ref.at[part[h]], raw1[p].at[part[h]],
             near_send.at[7 * p + h], near_recv.at[7 * p + h], at_offset(sign[p], 0),
         )
 
@@ -136,30 +136,35 @@
             far_send.at[o * side + i], far_recv.at[o * side + i], at_offset(0, ranked(i)),
         )
 
-    def spread(o):
+    def prepare(o):
         def one(i, carry):
-            if o < 5:
-                stage[o, i] = pick(sources[o], o, at_offset(0, ranked(i)))
+            stage[o, i] = pick(sources[o], o, at_offset(0, ranked(i)))
+            return carry
+
+        lax.fori_loop(1, side, one, 0)
+        recv[o * side] = pick(sources[o], o, me)
+
+    def spread(o, start=1):
+        def one(i, carry):
             across_v(o, i).start()
             return carry
 
-        lax.fori_loop(1, side, one, 0)
-        if o < 5:
-            recv[o * side] = pick(sources[o], o, me)
-        elif o < 7:
+        lax.fori_loop(start, side, one, 0)
+        if o in (5, 6):
             recv[o * side] = land3[o - 5, side // 2]
-        else:
+        elif o == 7:
             recv[o * side] = land4[0, 0]
 
-    load_points.wait()
     pl.semaphore_wait(barrier, 4 + side - 1 + chips)
     both = (0, 1)
-    for p in both:
-        for d in (1, 2):
-            tell(p, d).start()
     for h in both:
         for p in both:
             hop1(p, h).start()
+    for p in both:
+        for d in (1, 2):
+            tell(p, d).start()
+    load_points.wait()
+    prepare(0)
     acc[...] = jnp.zeros_like(acc)
     load_centroids.wait()
     for h in both:
@@ -167,31 +172,43 @@
             hop1(p, h).wait_recv()
             hop2(p, h).start()
     for p in both:
+        tell(p, 1).wait_recv()
+        prepare(1 + p)
+    for p in both:
         tell(p, 2).wait_recv()
         hop2(p, 0).wait_recv()
         hop2(p, 1).wait_recv()
 
+    fillers = 2
+    for i in range(1, 1 + fillers):
+        across_v(0, i).start()
+
+    for p in both:
+
         def beyond(i, carry):
             k = at_offset(2 * sign[p], ranked(p * (side // 2) + i))
             picked[p, i] = pick(raw2[p], 3 + p, k)
             return carry
 
+        lax.fori_loop(0, side // 2, beyond, 0)
+        hop3(p, 0).start()
+    for p in both:
+
         def following(i, carry):
             k = at_offset(sign[p], ranked(i))
             picked[p, side // 2 + i] = pick(raw2[p], 3 + p, k)
             return carry
 
-        lax.fori_loop(0, side // 2, beyond, 0)
-        hop3(p, 0).start()
         lax.fori_loop(0, side, following, 0)
         hop3(p, 1).start()
     for p in both:
+        prepare(3 + p)
+    for p in both:
         hop3(p, 0).wait_recv()
         hop4(p).start()
     for p in both:
-        tell(p, 1).wait_recv()
         hop3(p, 1).wait_recv()
-    spread(0)
+    spread(0, 1 + fillers)
     spread(1)
     for p in both:
         hop4(p).wait_recv()

time: 205 us -> 202 us (0.985)
  no operation moved by 1% of the time
where the time goes in v6:
time: 202 us
  Pallas kernels  200 us (99%)
    pallas_call x1, Pallas kernels, local(): pl.pallas_call(functools.partial(kernel, (slots, side, copies)), out_shap...  200 us

profile of v6, /device:TPU:1, one launch (start us, length us, event | category | flops | bytes accessed | tf_op | source)
XLA Modules:
  0.0 201.9 jit_solution(12957278011739206379)
XLA Ops:
  0.7 199.5 %shard_map.46 = bf16[256,512]{1,0:T(8,128)(2,1)} custom-call(s32[16]{0:T(128)} %ids_ref.1, s32[1]{0:T(128)S(6)} %copy.6.count_ref, bf16[16,128,512]{2,1,0:T(8,128)(2,1)} %points_ref.1, bf16[2048,512]{1,0:T(8,128)(2,1)} %centroids_ref.1), custom_call_target="tpu_custom_call" | custom-call | tf_op jit(solution)/shard_map/pallas_call | solution.py:356
  200.2 1.7 copy.7

commit v7 on v6

--- a/solution.py
+++ b/solution.py
@@ -38,7 +38,8 @@
         return (1 - core) * (a * side + b) + core * (b * side + a)
 
     def ranked(i):
-        return jnp.where(i % 2 == 1, (i + 1) // 2, (side - i // 2) % side)
+        far = jnp.where(i % 2 == 1, side // 2 - i // 2, side // 2 + i // 2)
+        return jnp.where(i == 0, 0, far)
 
     load_points = pltpu.make_async_copy(points_ref, pts_ref, load_sem.at[0])
     load_centroids = pltpu.make_async_copy(centroids_ref, cent_ref, load_sem.at[1])
@@ -144,12 +145,12 @@
         lax.fori_loop(1, side, one, 0)
         recv[o * side] = pick(sources[o], o, me)
 
-    def spread(o, start=1):
+    def spread(o, stop=side):
         def one(i, carry):
             across_v(o, i).start()
             return carry
 
-        lax.fori_loop(start, side, one, 0)
+        lax.fori_loop(1, stop, one, 0)
         if o in (5, 6):
             recv[o * side] = land3[o - 5, side // 2]
         elif o == 7:
@@ -180,7 +181,7 @@
         hop2(p, 1).wait_recv()
 
     fillers = 2
-    for i in range(1, 1 + fillers):
+    for i in range(side - fillers, side):
         across_v(0, i).start()
 
     for p in both:
@@ -208,7 +209,7 @@
         hop4(p).start()
     for p in both:
         hop3(p, 1).wait_recv()
-    spread(0, 1 + fillers)
+    spread(0, side - fillers)
     spread(1)
     for p in both:
         hop4(p).wait_recv()

time: 202 us -> 203 us (level)
  no operation moved by 1% of the time
where the time goes in v7:
time: 203 us
  Pallas kernels  201 us (99%)
    pallas_call x1, Pallas kernels, local(): pl.pallas_call(functools.partial(kernel, (slots, side, copies)), out_shap...  201 us

profile of v7, /device:TPU:1, one launch (start us, length us, event | category | flops | bytes accessed | tf_op | source)
XLA Modules:
  0.0 202.9 jit_solution(17356580013826112082)
XLA Ops:
  0.7 200.6 %shard_map.46 = bf16[256,512]{1,0:T(8,128)(2,1)} custom-call(s32[16]{0:T(128)} %ids_ref.1, s32[1]{0:T(128)S(6)} %copy.6.count_ref, bf16[16,128,512]{2,1,0:T(8,128)(2,1)} %points_ref.1, bf16[2048,512]{1,0:T(8,128)(2,1)} %centroids_ref.1), custom_call_target="tpu_custom_call" | custom-call | tf_op jit(solution)/shard_map/pallas_call | solution.py:357
  201.2 1.7 copy.7

commit v8 on v6

--- a/solution.py
+++ b/solution.py
@@ -179,7 +179,7 @@
         hop2(p, 0).wait_recv()
         hop2(p, 1).wait_recv()
 
-    fillers = 2
+    fillers = 4
     for i in range(1, 1 + fillers):
         across_v(0, i).start()
 

time: 202 us -> 203 us (level)
  no operation moved by 1% of the time
where the time goes in v8:
time: 203 us
  Pallas kernels  201 us (99%)
    pallas_call x1, Pallas kernels, local(): pl.pallas_call(functools.partial(kernel, (slots, side, copies)), out_shap...  201 us

profile of v8, /device:TPU:1, one launch (start us, length us, event | category | flops | bytes accessed | tf_op | source)
XLA Modules:
  0.0 202.9 jit_solution(4017765847385285870)
XLA Ops:
  0.7 200.5 %shard_map.46 = bf16[256,512]{1,0:T(8,128)(2,1)} custom-call(s32[16]{0:T(128)} %ids_ref.1, s32[1]{0:T(128)S(6)} %copy.6.count_ref, bf16[16,128,512]{2,1,0:T(8,128)(2,1)} %points_ref.1, bf16[2048,512]{1,0:T(8,128)(2,1)} %centroids_ref.1), custom_call_target="tpu_custom_call" | custom-call | tf_op jit(solution)/shard_map/pallas_call | solution.py:356
  201.2 1.7 copy.7
